TPU v7x, 32 devices: a whole 2x2x4 slice. The times are simulated.
32 devices in a mesh: row: 8 (over z, x), col: 4 (over y, core).
Axes of the slice: x: 2, y: 2, z: 4, core: 2. Of those that a mesh axis runs over, the one named last changes fastest.
Arguments:
- features: bfloat16 [14336, 2048], P('row', 'col'), may hold values from -6 to 6
- neighbours: int32 [14336, 32], P('row'), may hold values from -1 to 127, as said below
- node_valid: int32 [14336], P('row'), may hold values from 0 to 1, as said below
- weight_one: bfloat16 [2048, 2048], P(None, 'col'), may hold values from -0.125 to 0.125
- gamma_one: float32 [2048], P('col'), may hold values from 0.25 to 1.75
- beta_one: float32 [2048], P('col'), may hold values from -0.5 to 0.5
- weight_two: bfloat16 [2048, 2048], P(None, 'col'), may hold values from -0.125 to 0.125
- gamma_two: float32 [2048], P('col'), may hold values from 0.25 to 1.75
- beta_two: float32 [2048], P('col'), may hold values from -0.5 to 0.5
- cotangent: bfloat16 [14336, 2048], P('row', 'col'), may hold values from -6 to 6
Outputs:
- output: float32 [14336, 2048], P('row', 'col')
- grad_features: float32 [14336, 2048], P('row', 'col')
- grad_weight_one: float32 [2048, 2048], P(None, 'col')
- grad_gamma_one: float32 [2048], P('col')
- grad_beta_one: float32 [2048], P('col')
- grad_weight_two: float32 [2048, 2048], P(None, 'col')
- grad_gamma_two: float32 [2048], P('col')
- grad_beta_two: float32 [2048], P('col')
Inputs may be any that keep to these rules, and one draw needn't show every extreme that they name: `neighbours`: entries >= 0 name valid nodes of the same slot; every valid node has 1 to 32 such entries, first in its list, the rest are -1; a padding row has only -1; some slot is full. `node_valid`: in each slot the valid nodes come first and number at least 40.
All inputs are finite; a program needn't handle non-finite values.
Results may differ from a plain program's by a relative error of at most 0.012.
Values may be sent and summed in bfloat16 or wider, within the bound.
No kernel may reach another device: no remote copies, remote signals or barrier semaphores. Data moves between devices by JAX's collectives and lax.ppermute only.
A program may use at most 128 MiB of HBM per device.

v0:
```python
import jax
import jax.numpy as jnp
from jax import lax
from jax.sharding import PartitionSpec as P

SLOT = 128
NBR = 32
EPSILON = 1e-05


def build_tiles(neighbours):
    entries_all = neighbours.reshape(-1, SLOT, NBR)

    def build(entries):
        columns = jnp.arange(SLOT, dtype=jnp.int32)
        hits = jnp.sum((entries[:, :, None] == columns[None, None, :]).astype(jnp.float32), axis=1)
        degree = jnp.sum((entries >= 0).astype(jnp.float32), axis=1)
        joined = hits + jnp.eye(SLOT, dtype=jnp.float32)
        return joined / (degree[:, None] + 1.0)

    tiles = lax.map(build, entries_all)
    return (tiles, jnp.diagonal(tiles, axis1=1, axis2=2))


def spread(values, tiles, self_weight):
    shaped = values.reshape(tiles.shape[0], SLOT, values.shape[1])
    summed = jnp.einsum("sij,sjd->sid", tiles, shaped, precision=lax.Precision.HIGHEST)
    return (summed + self_weight[:, :, None] * shaped).reshape(values.shape)


def spread_back(grads, tiles, self_weight):
    shaped = grads.reshape(tiles.shape[0], SLOT, grads.shape[1])
    summed = jnp.einsum("sji,sjd->sid", tiles, shaped, precision=lax.Precision.HIGHEST)
    return (summed + self_weight[:, :, None] * shaped).reshape(grads.shape)


def moments(linear, valid):
    total_valid, summed = lax.psum((jnp.sum(valid), jnp.sum(valid * linear, axis=0)), "row")
    mean = summed / total_valid
    centred = linear - mean
    variance = lax.psum(jnp.sum(valid * centred * centred, axis=0), "row") / total_valid
    return (total_valid, mean, variance)


def forward_layer(values, weight, gamma, beta, tiles, self_weight, valid):
    mixed = spread(values, tiles, self_weight).astype(jnp.bfloat16)
    gathered = lax.all_gather(mixed, "col", axis=1, tiled=True)
    linear = jnp.dot(gathered, weight, preferred_element_type=jnp.float32)
    total_valid, mean, variance = moments(linear, valid)
    inv_std = lax.rsqrt(variance + EPSILON)
    normed = (linear - mean) * inv_std
    before = gamma * normed + beta
    result = valid * jax.nn.silu(before)
    return (result, (gathered, normed, inv_std, before, total_valid))


def backward_layer(grad_result, weight, gamma, kept, tiles, self_weight, valid):
    gathered, normed, inv_std, before, total_valid = kept
    sigmoid_value = jax.nn.sigmoid(before)
    slope = sigmoid_value * (1.0 + before * (1.0 - sigmoid_value))
    grad_before = grad_result * valid * slope
    grad_beta, grad_gamma = lax.psum(
        (jnp.sum(grad_before, axis=0), jnp.sum(grad_before * normed, axis=0)), "row"
    )
    grad_normed = gamma * grad_before
    grad_linear = inv_std * (
        grad_normed - valid * (gamma * grad_beta + normed * gamma * grad_gamma) / total_valid
    )
    grad_low = grad_linear.astype(jnp.bfloat16)
    weight_terms = lax.dot_general(
        gathered, grad_low, (((0,), (0,)), ((), ())), preferred_element_type=jnp.float32
    )
    grad_weight = lax.psum(weight_terms, "row")
    partial_terms = lax.dot_general(
        grad_low, weight, (((1,), (1,)), ((), ())), preferred_element_type=jnp.float32
    )
    grad_mixed = lax.psum_scatter(partial_terms, "col", scatter_dimension=1, tiled=True)
    grad_values = spread_back(grad_mixed, tiles, self_weight)
    return (grad_values, grad_weight, grad_gamma, grad_beta)


def local(
    features,
    neighbours,
    node_valid,
    weight_one,
    gamma_one,
    beta_one,
    weight_two,
    gamma_two,
    beta_two,
    cotangent,
):
    tiles, self_weight = build_tiles(neighbours)
    valid = node_valid.astype(jnp.float32)[:, None]
    hidden, kept_one = forward_layer(
        features.astype(jnp.float32), weight_one, gamma_one, beta_one, tiles, self_weight, valid
    )
    output, kept_two = forward_layer(
        hidden, weight_two, gamma_two, beta_two, tiles, self_weight, valid
    )
    grad_hidden, grad_weight_two, grad_gamma_two, grad_beta_two = backward_layer(
        cotangent.astype(jnp.float32), weight_two, gamma_two, kept_two, tiles, self_weight, valid
    )
    grad_features, grad_weight_one, grad_gamma_one, grad_beta_one = backward_layer(
        grad_hidden, weight_one, gamma_one, kept_one, tiles, self_weight, valid
    )
    return (
        output,
        grad_features,
        grad_weight_one,
        grad_gamma_one,
        grad_beta_one,
        grad_weight_two,
        grad_gamma_two,
        grad_beta_two,
    )


def solution(mesh):
    placed = (
        P("row", "col"),
        P("row", None),
        P("row"),
        P(None, "col"),
        P("col"),
        P("col"),
        P(None, "col"),
        P("col"),
        P("col"),
        P("row", "col"),
    )
    return jax.shard_map(
        local,
        mesh=mesh,
        in_specs=placed,
        out_specs=(
            P("row", "col"),
            P("row", "col"),
            P(None, "col"),
            P("col"),
            P("col"),
            P(None, "col"),
            P("col"),
            P("col"),
        ),
        check_vma=False,
    )
```

profile of v0, /device:TPU:0, one launch (start us, length us, event | category | flops | bytes accessed | tf_op | source)
XLA Modules:
  0.0 855.5 jit_solution(2408295498759646820)
XLA Ops:
  9.6 27.6 %while.10 = (s32[]{:T(128)}, f32[14,128,128]{2,1,0:T(8,128)S(1)}, s32[14,128,32]{2,1,0:T(8,128)}, s32[]{:T(128)}) while((s32[]{:T(128)}, f32[14,128,128]{2,1,0:T(8,128)S(1)}, s32[14,128,32]{2,1,0:T(8,128)}, s32[]{:T(128)}) %tuple.47), condition=%wide.region_3.4_spmd, body=%wide.region_0.3_spmd.sunk | while | flops 1634306 | bytes 247877 | solution.py:21
  43.7 5.1 add_convert_fusion.1
  49.5 54.5 %all-gather.3.cloned.1.call-done = bf16[1792,2048]{1,0:T(8,128)(2,1)} async-done(((bf16[1792,512]{1,0:T(8,128)(2,1)}), bf16[1792,2048]{1,0:T(8,128)(2,1)}) %all-gather.3.cloned.1.call-update) | async-done | bytes 7340048 | tf_op jit(solution)/shard_map/all_gather | solution.py:47
  104.0 9.5 %multiply_reduce_fusion.3 = (f32[512]{0:T(512)S(1)}, f32[1792,512]{1,0:T(8,128)}) fusion(f32[1792]{0:T(1024)S(1)} %convert_element_type.41, bf16[1792,2048]{1,0:T(8,128)(2,1)} %all-gather.3.cloned.1.call-done, bf16[2048,512]{1,0:T(8,128)(2,1)} %param.15), kind=kOutput, calls=%fused_computation.29 | convolution fusion | flops 3759930880 | bytes 13116416 | tf_op jit(solution)/shard_map/dot_general | solution.py:48
  113.5 22.0 %all-reduce.2 = (f32[512]{0:T(512)S(1)}, f32[]{:T(128)}) all-reduce(f32[512]{0:T(512)S(1)} %get-tuple-element.49, f32[]{:T(128)} %convert_reduce_fusion.2), channel_id=1, replica_groups=mesh['row'=8,'col'=4] {'row'}, use_global_device_ids=true, to_apply=%region_5.6 | all-reduce | flops 513 | bytes 4104 | tf_op jit(solution)/shard_map/psum | solution.py:38
  138.6 17.1 %psum.82 = f32[512]{0:T(512)S(1)} all-reduce(f32[512]{0:T(512)S(1)} %fusion.2), channel_id=1, replica_groups=mesh['row'=8,'col'=4] {'row'}, use_global_device_ids=true, to_apply=%region_9.10 | all-reduce | flops 512 | bytes 4096 | tf_op jit(solution)/shard_map/psum | solution.py:41
  164.1 50.0 %all-gather.5.cloned.1.call-done = bf16[1792,2048]{1,0:T(8,128)(2,1)} async-done(((bf16[1792,512]{1,0:T(8,128)(2,1)}), bf16[1792,2048]{1,0:T(8,128)(2,1)}) %all-gather.5.cloned.1.call-update) | async-done | bytes 7340048 | tf_op jit(solution)/shard_map/all_gather | solution.py:47
  214.1 8.9 %multiply_reduce_fusion.2 = (f32[512]{0:T(512)S(1)}, f32[1792,512]{1,0:T(8,128)}) fusion(f32[1792]{0:T(1024)S(1)} %convert_element_type.41, bf16[1792,2048]{1,0:T(8,128)(2,1)} %all-gather.5.cloned.1.call-done, bf16[2048,512]{1,0:T(8,128)(2,1)S(1)} %copy-done), kind=kOutput, calls=%fused_computation.25 | convolution fusion | flops 3759930880 | bytes 13116416 | tf_op jit(solution)/shard_map/dot_general | solution.py:48
  223.0 21.5 %psum.83 = f32[512]{0:T(512)S(1)} all-reduce(f32[512]{0:T(512)S(1)} %get-tuple-element.51), channel_id=1, replica_groups=mesh['row'=8,'col'=4] {'row'}, use_global_device_ids=true, to_apply=%region_11.12 | all-reduce | flops 512 | bytes 4096 | tf_op jit(solution)/shard_map/psum | solution.py:38
  247.7 17.1 %psum.84 = f32[512]{0:T(512)S(1)} all-reduce(f32[512]{0:T(512)S(1)} %fusion.3), channel_id=1, replica_groups=mesh['row'=8,'col'=4] {'row'}, use_global_device_ids=true, to_apply=%region_13.14 | all-reduce | flops 512 | bytes 4096 | tf_op jit(solution)/shard_map/psum | solution.py:41
  265.4 6.3 fusion.6
  271.7 19.1 %all-reduce.1 = (f32[512]{0:T(512)S(1)}, f32[512]{0:T(512)S(1)}) all-reduce(f32[512]{0:T(512)S(1)} %get-tuple-element.29, f32[512]{0:T(512)S(1)} %get-tuple-element.28), channel_id=1, replica_groups=mesh['row'=8,'col'=4] {'row'}, use_global_device_ids=true, to_apply=%region_17.18 | all-reduce | flops 1024 | bytes 8192 | tf_op jit(solution)/shard_map/psum | solution.py:62
  296.6 7.2 fusion.8
  304.1 109.0 %reduce-scatter.3.cloned.1.call-done = f32[1792,512]{1,0:T(8,128)} async-done(((f32[1792,2048]{1,0:T(8,128)}), f32[1792,512]{1,0:T(8,128)}) %reduce-scatter.3.cloned.1.call-update) | async-done | bytes 3670032 | tf_op jit(solution)/shard_map/reduce_scatter | solution.py:77
  413.1 6.8 multiply_add_fusion.1
  423.7 21.3 %all-reduce = (f32[512]{0:T(512)S(1)}, f32[512]{0:T(512)S(1)}) all-reduce(f32[512]{0:T(512)S(1)} %get-tuple-element.27, f32[512]{0:T(512)S(1)} %get-tuple-element.26), channel_id=1, replica_groups=mesh['row'=8,'col'=4] {'row'}, use_global_device_ids=true, to_apply=%region_22.23 | all-reduce | flops 1024 | bytes 8192 | tf_op jit(solution)/shard_map/psum | solution.py:62
  445.0 4.7 multiply_convert_fusion
  449.8 7.3 fusion.9
  458.5 9.9 %fusion.11 = f32[2048,512]{1,0:T(8,128)} fusion(bf16[1792,2048]{1,0:T(8,128)(2,1)} %all-gather.5.cloned.1.call-done, bf16[1792,512]{1,0:T(8,128)(2,1)S(1)} %copy-done.5), kind=kOutput, calls=%fused_computation.44 | convolution fusion | flops 3758096384 | bytes 13369344 | tf_op jit(solution)/shard_map/dot_general | solution.py:70
  468.4 10.5 %fusion.10 = f32[2048,512]{1,0:T(8,128)} fusion(bf16[1792,2048]{1,0:T(8,128)(2,1)} %all-gather.3.cloned.1.call-done, bf16[1792,512]{1,0:T(8,128)(2,1)S(1)} %copy-done.7), kind=kOutput, calls=%fused_computation.43 | convolution fusion | flops 3758096384 | bytes 13369344 | tf_op jit(solution)/shard_map/dot_general | solution.py:70
  479.0 87.5 %reduce-scatter.5.cloned.1.call-done = f32[1792,512]{1,0:T(8,128)} async-done(((f32[1792,2048]{1,0:T(8,128)}), f32[1792,512]{1,0:T(8,128)}) %reduce-scatter.5.cloned.1.call-update) | async-done | bytes 3670032 | tf_op jit(solution)/shard_map/reduce_scatter | solution.py:77
  566.5 8.5 multiply_add_fusion
  575.0 267.1 %all-reduce.6.cloned.1.call-done = (f32[2048,512]{1,0:T(8,128)}, f32[2048,512]{1,0:T(8,128)}) async-done(((f32[2048,512]{1,0:T(8,128)}, f32[2048,512]{1,0:T(8,128)}), (f32[2048,512]{1,0:T(8,128)}, f32[2048,512]{1,0:T(8,128)})) %all-reduce.6.cloned.1.call-update) | async-done | bytes 8388624 | tf_op jit(solution)/shard_map/psum | solution.py:73
  842.1 4.8 copy.41
  (123 shorter events, 65.0 us)
Async XLA Ops:
  7.2 207.0 %copy-start = (bf16[2048,512]{1,0:T(8,128)(2,1)S(1)}, bf16[2048,512]{1,0:T(8,128)(2,1)}, u32[]{:S(2)}) copy-start(bf16[2048,512]{1,0:T(8,128)(2,1)} %param.18) | copy-start | bytes 6291460
  7.2 96.8 %all-gather.3.cloned.1.call-start = ((), (), s32[]{:S(2)}) async-start(), calls=%async_computation.2 | async-start | bytes 9175040 | tf_op jit(solution)/shard_map/all_gather | solution.py:47
  41.8 7.0 copy-start.8
  48.8 165.3 %all-gather.5.cloned.1.call-start = ((), (), s32[]{:S(2)}) async-start(), calls=%async_computation.3 | async-start | bytes 9175040 | tf_op jit(solution)/shard_map/all_gather | solution.py:47
  113.5 42.8 %copy-start.9 = (f32[512]{0:T(512)S(1)}, f32[512]{0:T(512)}, u32[]{:S(2)}) copy-start(f32[512]{0:T(512)} %param.16) | copy-start | bytes 6148
  113.5 42.8 %copy-start.11 = (f32[512]{0:T(512)S(1)}, f32[512]{0:T(512)}, u32[]{:S(2)}) copy-start(f32[512]{0:T(512)} %param.17) | copy-start | bytes 6148
  163.9 249.3 %reduce-scatter.3.cloned.1.call-start = ((), (), s32[]{:S(2)}) async-start(), calls=%async_computation.4 | async-start | bytes 18350080 | tf_op jit(solution)/shard_map/reduce_scatter | solution.py:77
  223.0 42.3 %copy-start.10 = (f32[512]{0:T(512)S(1)}, f32[512]{0:T(512)}, u32[]{:S(2)}) copy-start(f32[512]{0:T(512)} %param.19) | copy-start | bytes 6148
  223.0 42.3 %copy-start.12 = (f32[512]{0:T(512)S(1)}, f32[512]{0:T(512)}, u32[]{:S(2)}) copy-start(f32[512]{0:T(512)} %param.20) | copy-start | bytes 6148
  290.8 4.5 copy-start.13
  290.8 4.6 copy-start.15
  295.3 1.2 copy-start.4
  303.8 262.6 %reduce-scatter.5.cloned.1.call-start = ((), (), s32[]{:S(2)}) async-start(), calls=%async_computation.5 | async-start | bytes 18350080 | tf_op jit(solution)/shard_map/reduce_scatter | solution.py:77
  413.1 6.8 copy-start.2
  445.0 4.7 copy-start.14
  445.0 4.7 copy-start.16
  445.0 4.7 copy-start.17
  449.7 7.3 copy-start.6
  457.0 1.5 copy-start.5
  457.0 385.1 %all-reduce.6.cloned.1.call-start = ((), (), s32[]{:S(2)}) async-start(), calls=%async_computation.6 | async-start | bytes 16777216 | tf_op jit(solution)/shard_map/psum | solution.py:73
  458.5 9.9 %copy-start.7 = (bf16[1792,512]{1,0:T(8,128)(2,1)S(1)}, bf16[1792,512]{1,0:T(8,128)(2,1)}, u32[]{:S(2)}) copy-start(bf16[1792,512]{1,0:T(8,128)(2,1)} %copy-done.6) | copy-start | bytes 5505028
  842.1 4.8 copy-start.3
  842.1 6.8 copy-start.1
Sparse Core Ops, SparseCore 0:
  48.9 55.0 all-gather.2
  164.0 50.1 all-gather.4
  303.9 109.1 reduce-scatter.2
  457.2 109.2 reduce-scatter.4
  571.0 271.0 all-reduce.5
where the time goes:
time: 857 us; the launch traced here: 855 us
  waiting for transfers between devices  568 us (66%)
  blocking collectives  118 us (14%)
  matrix products  78.2 us (9%)
  other arithmetic  57.2 us (7%)
  local copies, waits for them, and re-layouts  18.1 us (2%)
  between operations  14 us (2%)
    psum x1, waiting for transfers between devices, backward_layer(): grad_weight = lax.psum(weight_terms, 'row')  267 us
    reduce_scatter x2, waiting for transfers between devices, backward_layer(): lax.psum_scatter(partial_terms, 'col', scatter_dimension=1, tiled=True)  197 us
    all_gather x2, waiting for transfers between devices, forward_layer(): gathered = lax.all_gather(mixed, 'col', axis=1, tiled=True)  105 us
    psum x2, blocking collectives, moments(): lax.psum((jnp.sum(valid), jnp.sum(valid * linear, axis=0)), 'row')  43.4 us
    psum x2, blocking collectives, backward_layer(): lax.psum((jnp.sum(grad_before, axis=0), jnp.sum(grad_before * normed, axi...  40.5 us
    psum x2, blocking collectives, moments(): lax.psum(jnp.sum(valid * centred * centred, axis=0), 'row') / total_valid  34.3 us
    dot_general x2, matrix products, backward_layer(): lax.dot_general(gathered, grad_low, (((0,), (0,)), ((), ())), preferred_e...  20.4 us
    dot_general x2, matrix products, forward_layer(): linear = jnp.dot(gathered, weight, preferred_element_type=jnp.float32)  18.4 us
  transfers between devices with their start and end apart: 5, of which 5 were waited for; matrix products, arithmetic and copies ran while one was open for 3% of the time, Pallas kernels for 0%

commit v1 on v0

--- a/solution.py
+++ b/solution.py
@@ -70,7 +70,11 @@
     weight_terms = lax.dot_general(
         gathered, grad_low, (((0,), (0,)), ((), ())), preferred_element_type=jnp.float32
     )
-    grad_weight = lax.psum(weight_terms, "row")
+    grad_weight = weight_terms
+    for hop in (1, 2, 4):
+        grad_weight = grad_weight + lax.ppermute(
+            grad_weight, "row", [(dev, dev ^ hop) for dev in range(8)]
+        )
     partial_terms = lax.dot_general(
         grad_low, weight, (((1,), (1,)), ((), ())), preferred_element_type=jnp.float32
     )

time: 857 us -> 1030 us (1.20)
  waiting for transfers between devices: 568 us -> 734 us
    ppermute x0 -> x6, waiting for transfers between devices: none -> 520 us  [backward_layer(): lax.ppermute(grad_weight, 'row', [(dev, dev ^ hop) for dev in range(8)])]
    psum x1 -> x0, waiting for transfers between devices: 267 us -> none  [backward_layer(): grad_weight = lax.psum(weight_terms, 'row')]
    reduce_scatter x2, waiting for transfers between devices: 197 us -> 109 us  [backward_layer(): lax.psum_scatter(partial_terms, 'col', scatter_dimension=1, tiled=True)]
  transfers between devices with their start and end apart: 5 -> 10, of which waited for: 5 -> 8; matrix products, arithmetic and copies ran while one was open for 3% -> 2% of each run, Pallas kernels for 0% -> 0%
where the time goes in v1:
time: 1030 us; the launch traced here: 1020 us
  waiting for transfers between devices  734 us (71%)
  blocking collectives  118 us (11%)
  matrix products  72.1 us (7%)
  other arithmetic  67.4 us (7%)
  between operations  14.3 us (1%)
  local copies, waits for them, and re-layouts  11.6 us (1%)
    ppermute x6, waiting for transfers between devices, backward_layer(): lax.ppermute(grad_weight, 'row', [(dev, dev ^ hop) for dev in range(8)])  520 us
    reduce_scatter x2, waiting for transfers between devices, backward_layer(): lax.psum_scatter(partial_terms, 'col', scatter_dimension=1, tiled=True)  109 us
    all_gather x2, waiting for transfers between devices, forward_layer(): gathered = lax.all_gather(mixed, 'col', axis=1, tiled=True)  104 us
    psum x2, blocking collectives, moments(): lax.psum((jnp.sum(valid), jnp.sum(valid * linear, axis=0)), 'row')  43.5 us
    psum x2, blocking collectives, backward_layer(): lax.psum((jnp.sum(grad_before, axis=0), jnp.sum(grad_before * normed, axi...  40.5 us
    psum x2, blocking collectives, moments(): lax.psum(jnp.sum(valid * centred * centred, axis=0), 'row') / total_valid  34.3 us
  transfers between devices with their start and end apart: 10, of which 8 were waited for; matrix products, arithmetic and copies ran while one was open for 2% of the time, Pallas kernels for 0%

profile of v1, /device:TPU:0, one launch (start us, length us, event | category | flops | bytes accessed | tf_op | source)
XLA Modules:
  0.0 1021.7 jit_solution(17962713680265296360)
XLA Ops:
  9.6 27.6 %while.10 = (s32[]{:T(128)}, f32[14,128,128]{2,1,0:T(8,128)S(1)}, s32[14,128,32]{2,1,0:T(8,128)}, s32[]{:T(128)}) while((s32[]{:T(128)}, f32[14,128,128]{2,1,0:T(8,128)S(1)}, s32[14,128,32]{2,1,0:T(8,128)}, s32[]{:T(128)}) %tuple.43), condition=%wide.region_3.4_spmd, body=%wide.region_0.3_spmd.sunk | while | flops 1634306 | bytes 247877 | solution.py:21
  49.5 54.5 %all-gather.3.cloned.1.call-done = bf16[1792,2048]{1,0:T(8,128)(2,1)} async-done(((bf16[1792,512]{1,0:T(8,128)(2,1)}), bf16[1792,2048]{1,0:T(8,128)(2,1)}) %all-gather.3.cloned.1.call-update) | async-done | bytes 7340048 | tf_op jit(solution)/shard_map/all_gather | solution.py:47
  104.0 9.5 multiply_reduce_fusion.3
  113.5 22.0 %all-reduce.2 = (f32[512]{0:T(512)S(1)}, f32[]{:T(128)}) all-reduce(f32[512]{0:T(512)S(1)} %get-tuple-element.47, f32[]{:T(128)} %convert_reduce_fusion.2), channel_id=1, replica_groups=mesh['row'=8,'col'=4] {'row'}, use_global_device_ids=true, to_apply=%region_5.6 | all-reduce | flops 513 | bytes 4104 | tf_op jit(solution)/shard_map/psum | solution.py:38
  138.6 17.1 %psum.68 = f32[512]{0:T(512)S(1)} all-reduce(f32[512]{0:T(512)S(1)} %fusion.2), channel_id=1, replica_groups=mesh['row'=8,'col'=4] {'row'}, use_global_device_ids=true, to_apply=%region_9.10 | all-reduce | flops 512 | bytes 4096 | tf_op jit(solution)/shard_map/psum | solution.py:41
  164.4 49.8 %all-gather.5.cloned.1.call-done = bf16[1792,2048]{1,0:T(8,128)(2,1)} async-done(((bf16[1792,512]{1,0:T(8,128)(2,1)}), bf16[1792,2048]{1,0:T(8,128)(2,1)}) %all-gather.5.cloned.1.call-update) | async-done | bytes 7340048 | tf_op jit(solution)/shard_map/all_gather | solution.py:47
  214.1 8.9 multiply_reduce_fusion.2
  223.0 21.5 %psum.69 = f32[512]{0:T(512)S(1)} all-reduce(f32[512]{0:T(512)S(1)} %get-tuple-element.49), channel_id=1, replica_groups=mesh['row'=8,'col'=4] {'row'}, use_global_device_ids=true, to_apply=%region_11.12 | all-reduce | flops 512 | bytes 4096 | tf_op jit(solution)/shard_map/psum | solution.py:38
  247.7 17.1 %psum.70 = f32[512]{0:T(512)S(1)} all-reduce(f32[512]{0:T(512)S(1)} %fusion.3), channel_id=1, replica_groups=mesh['row'=8,'col'=4] {'row'}, use_global_device_ids=true, to_apply=%region_13.14 | all-reduce | flops 512 | bytes 4096 | tf_op jit(solution)/shard_map/psum | solution.py:41
  265.4 6.3 fusion.6
  271.7 19.1 %all-reduce.1 = (f32[512]{0:T(512)S(1)}, f32[512]{0:T(512)S(1)}) all-reduce(f32[512]{0:T(512)S(1)} %get-tuple-element.29, f32[512]{0:T(512)S(1)} %get-tuple-element.28), channel_id=1, replica_groups=mesh['row'=8,'col'=4] {'row'}, use_global_device_ids=true, to_apply=%region_17.18 | all-reduce | flops 1024 | bytes 8192 | tf_op jit(solution)/shard_map/psum | solution.py:62
  296.6 7.2 fusion.8
  304.1 109.1 %reduce-scatter.3.cloned.1.call-done = f32[1792,512]{1,0:T(8,128)} async-done(((f32[1792,2048]{1,0:T(8,128)}), f32[1792,512]{1,0:T(8,128)}) %reduce-scatter.3.cloned.1.call-update) | async-done | bytes 3670032 | tf_op jit(solution)/shard_map/reduce_scatter | solution.py:81
  413.1 6.8 multiply_add_fusion.1
  423.7 21.3 %all-reduce = (f32[512]{0:T(512)S(1)}, f32[512]{0:T(512)S(1)}) all-reduce(f32[512]{0:T(512)S(1)} %get-tuple-element.27, f32[512]{0:T(512)S(1)} %get-tuple-element.26), channel_id=1, replica_groups=mesh['row'=8,'col'=4] {'row'}, use_global_device_ids=true, to_apply=%region_22.23 | all-reduce | flops 1024 | bytes 8192 | tf_op jit(solution)/shard_map/psum | solution.py:62
  449.8 7.3 fusion.9
  458.5 6.9 fusion.11
  465.6 7.3 fusion.10
  475.0 84.0 %collective-permute-done.3 = f32[2048,512]{1,0:T(8,128)S(1)} collective-permute-done((f32[2048,512]{1,0:T(8,128)S(1)}, f32[2048,512]{1,0:T(8,128)S(1)}, u32[]{:S(2)}, u32[]{:S(2)}) %collective-permute-start.3) | collective-permute-done | bytes 4194336 | tf_op jit(solution)/shard_map/ppermute | solution.py:75
  560.1 83.3 %collective-permute-done = f32[2048,512]{1,0:T(8,128)S(1)} collective-permute-done((f32[2048,512]{1,0:T(8,128)S(1)}, f32[2048,512]{1,0:T(8,128)S(1)}, u32[]{:S(2)}, u32[]{:S(2)}) %collective-permute-start) | collective-permute-done | bytes 4194336 | tf_op jit(solution)/shard_map/ppermute | solution.py:75
  645.6 172.2 %collective-permute-done.1 = f32[2048,512]{1,0:T(8,128)S(1)} collective-permute-done((f32[2048,512]{1,0:T(8,128)S(1)}, f32[2048,512]{1,0:T(8,128)S(1)}, u32[]{:S(2)}, u32[]{:S(2)}) %collective-permute-start.1) | collective-permute-done | bytes 4194336 | tf_op jit(solution)/shard_map/ppermute | solution.py:75
  819.4 97.7 %collective-permute-done.5 = f32[2048,512]{1,0:T(8,128)S(1)} collective-permute-done((f32[2048,512]{1,0:T(8,128)S(1)}, f32[2048,512]{1,0:T(8,128)S(1)}, u32[]{:S(2)}, u32[]{:S(2)}) %collective-permute-start.5) | collective-permute-done | bytes 4194336 | tf_op jit(solution)/shard_map/ppermute | solution.py:75
  920.1 83.2 %collective-permute-done.2 = f32[2048,512]{1,0:T(8,128)S(1)} collective-permute-done((f32[2048,512]{1,0:T(8,128)S(1)}, f32[2048,512]{1,0:T(8,128)S(1)}, u32[]{:S(2)}, u32[]{:S(2)}) %collective-permute-start.2) | collective-permute-done | bytes 4194336 | tf_op jit(solution)/shard_map/ppermute | solution.py:75
  1006.4 8.6 multiply_add_fusion
  (134 shorter events, 86.1 us)
Async XLA Ops:
  7.2 207.0 %copy-start = (bf16[2048,512]{1,0:T(8,128)(2,1)S(1)}, bf16[2048,512]{1,0:T(8,128)(2,1)}, u32[]{:S(2)}) copy-start(bf16[2048,512]{1,0:T(8,128)(2,1)} %param.18) | copy-start | bytes 6291460
  7.2 96.8 %all-gather.3.cloned.1.call-start = ((), (), s32[]{:S(2)}) async-start(), calls=%async_computation.2 | async-start | bytes 9175040 | tf_op jit(solution)/shard_map/all_gather | solution.py:47
  41.8 7.0 copy-start.7
  48.8 165.3 %all-gather.5.cloned.1.call-start = ((), (), s32[]{:S(2)}) async-start(), calls=%async_computation.3 | async-start | bytes 9175040 | tf_op jit(solution)/shard_map/all_gather | solution.py:47
  113.5 42.8 %copy-start.8 = (f32[512]{0:T(512)S(1)}, f32[512]{0:T(512)}, u32[]{:S(2)}) copy-start(f32[512]{0:T(512)} %param.16) | copy-start | bytes 6148
  113.5 42.8 %copy-start.10 = (f32[512]{0:T(512)S(1)}, f32[512]{0:T(512)}, u32[]{:S(2)}) copy-start(f32[512]{0:T(512)} %param.17) | copy-start | bytes 6148
  163.9 249.3 %reduce-scatter.3.cloned.1.call-start = ((), (), s32[]{:S(2)}) async-start(), calls=%async_computation.4 | async-start | bytes 18350080 | tf_op jit(solution)/shard_map/reduce_scatter | solution.py:81
  223.0 42.3 %copy-start.9 = (f32[512]{0:T(512)S(1)}, f32[512]{0:T(512)}, u32[]{:S(2)}) copy-start(f32[512]{0:T(512)} %param.19) | copy-start | bytes 6148
  223.0 42.4 %copy-start.11 = (f32[512]{0:T(512)S(1)}, f32[512]{0:T(512)}, u32[]{:S(2)}) copy-start(f32[512]{0:T(512)} %param.20) | copy-start | bytes 6148
  290.8 4.6 copy-start.14
  303.8 702.5 %reduce-scatter.5.cloned.1.call-start = ((), (), s32[]{:S(2)}) async-start(), calls=%async_computation.5 | async-start | bytes 18350080 | tf_op jit(solution)/shard_map/reduce_scatter | solution.py:81
  413.1 6.8 copy-start.2
  445.0 4.7 copy-start.13
  445.0 4.7 copy-start.15
  445.0 4.7 copy-start.16
  449.8 7.3 copy-start.5
  458.5 7.0 copy-start.6
  465.5 93.6 %collective-permute-start.3 = (f32[2048,512]{1,0:T(8,128)S(1)}, f32[2048,512]{1,0:T(8,128)S(1)}, u32[]{:S(2)}, u32[]{:S(2)}) collective-permute-start(f32[2048,512]{1,0:T(8,128)S(1)} %fusion.11), channel_id=1, source_target_pairs={{0,4},{4,0},{8,12},{12,8},{16,20},{20,16},{24,28},{28,24},{1,5},{5... | collective-permute-start | bytes 12582920 | tf_op jit(solution)/shard_map/ppermute | solution.py:75
  472.8 170.6 %collective-permute-start = (f32[2048,512]{1,0:T(8,128)S(1)}, f32[2048,512]{1,0:T(8,128)S(1)}, u32[]{:S(2)}, u32[]{:S(2)}) collective-permute-start(f32[2048,512]{1,0:T(8,128)S(1)} %fusion.10), channel_id=1, source_target_pairs={{0,4},{4,0},{8,12},{12,8},{16,20},{20,16},{24,28},{28,24},{1,5},{5... | collective-permute-start | bytes 12582920 | tf_op jit(solution)/shard_map/ppermute | solution.py:75
  560.1 84.5 %collective-permute-start.4 = (f32[2048,512]{1,0:T(8,128)S(1)}, f32[2048,512]{1,0:T(8,128)S(1)}, u32[]{:S(2)}, u32[]{:S(2)}) collective-permute-start(f32[2048,512]{1,0:T(8,128)S(1)} %add.152), channel_id=1, source_target_pairs={{0,8},{4,12},{8,0},{12,4},{16,24},{20,28},{24,16},{28,20},{1,9},{5... | collective-permute-start | bytes 12582920 | tf_op jit(solution)/shard_map/ppermute | solution.py:75
  644.4 173.4 %collective-permute-start.1 = (f32[2048,512]{1,0:T(8,128)S(1)}, f32[2048,512]{1,0:T(8,128)S(1)}, u32[]{:S(2)}, u32[]{:S(2)}) collective-permute-start(f32[2048,512]{1,0:T(8,128)S(1)} %add.149), channel_id=1, source_target_pairs={{0,8},{4,12},{8,0},{12,4},{16,24},{20,28},{24,16},{28,20},{1,9},{5... | collective-permute-start | bytes 12582920 | tf_op jit(solution)/shard_map/ppermute | solution.py:75
  645.6 271.5 %collective-permute-start.5 = (f32[2048,512]{1,0:T(8,128)S(1)}, f32[2048,512]{1,0:T(8,128)S(1)}, u32[]{:S(2)}, u32[]{:S(2)}) collective-permute-start(f32[2048,512]{1,0:T(8,128)S(1)} %add.153), channel_id=1, source_target_pairs={{0,16},{4,20},{8,24},{12,28},{16,0},{20,4},{24,8},{28,12},{1,17},{... | collective-permute-start | bytes 12582920 | tf_op jit(solution)/shard_map/ppermute | solution.py:75
  818.9 184.4 %collective-permute-start.2 = (f32[2048,512]{1,0:T(8,128)S(1)}, f32[2048,512]{1,0:T(8,128)S(1)}, u32[]{:S(2)}, u32[]{:S(2)}) collective-permute-start(f32[2048,512]{1,0:T(8,128)S(1)} %add.150), channel_id=1, source_target_pairs={{0,16},{4,20},{8,24},{12,28},{16,0},{20,4},{24,8},{28,12},{1,17},{... | collective-permute-start | bytes 12582920 | tf_op jit(solution)/shard_map/ppermute | solution.py:75
  1006.4 8.6 copy-start.1
  (3 other events, 7.3 us)
Sparse Core Ops, SparseCore 0:
  48.9 55.0 all-gather.2
  164.0 50.0 all-gather.4
  304.0 109.1 reduce-scatter.2
  457.2 109.2 reduce-scatter.4
